TPU v7x, 256 devices: a whole 4x4x8 slice. The times are simulated.
256 devices in a mesh: pipe: 8 (over x, core), seq: 32 (over z, y).
Axes of the slice: x: 4, y: 4, z: 8, core: 2. Of those that a mesh axis runs over, the one named last changes fastest.
Arguments:
- saved_inputs: bfloat16 [8, 2, 8192, 1536], P('pipe', None, 'seq'), may hold values from -54 to 54
- arrived_grad: bfloat16 [8, 8192, 1536], P('pipe', 'seq'), may hold values from -6 to 6
- loss_grad: bfloat16 [1, 8192, 1536], P(None, 'seq'), may hold values from -6 to 6
- norm_gain: float32 [8, 1536], P('pipe'), may hold values from 0.25 to 1.75
- w_gate: bfloat16 [8, 384, 1536], P('pipe'), may hold values from -0.3125 to 0.3125
- w_value: bfloat16 [8, 384, 1536], P('pipe'), may hold values from -0.3125 to 0.3125
- w_out: bfloat16 [8, 384, 1536], P('pipe'), may hold values from -0.3125 to 0.3125
- r_factor: bfloat16 [8, 8192, 256], P('pipe', 'seq'), may hold values from -0.375 to 0.375
- l_factor: bfloat16 [8, 256, 1024], P('pipe', 'seq'), may hold values from -1 to 1
Outputs:
- sent_grad: bfloat16 [8, 2, 8192, 1536], P('pipe', None, 'seq')
All inputs are finite; a program needn't handle non-finite values.
Results may differ from a plain program's by a relative error of at most 0.008.
Values may be sent and summed in bfloat16 or wider, within the bound.
A program may use at most 128 MiB of HBM per device.

v0:
```python
import jax
import jax.numpy as jnp
from jax import lax
from jax.sharding import PartitionSpec as P

TICKS = 2


epsilon = 1e-05


def from_behind(value, axis, steps):
    count = lax.axis_size(axis)
    initial, last = (max(0, -steps), min(count, count - steps))
    return lax.ppermute(value, axis, [(source, source + steps) for source in range(initial, last)])


def block_apply(rows_in, weight):
    row_count = rows_in.shape[0]
    block_width = weight.shape[0]
    left_blocks = rows_in.reshape(row_count, -1, block_width)
    right_blocks = weight.reshape(block_width, -1, block_width)
    return jnp.einsum(
        "rnc,cnb->rnb", left_blocks, right_blocks, preferred_element_type=jnp.float32
    ).reshape(row_count, -1)


def block_back(rows_in, weight):
    row_count = rows_in.shape[0]
    block_width = weight.shape[0]
    left_blocks = rows_in.reshape(row_count, -1, block_width)
    right_blocks = weight.reshape(block_width, -1, block_width)
    return jnp.einsum(
        "rnb,cnb->rnc", left_blocks, right_blocks, preferred_element_type=jnp.float32
    ).reshape(row_count, -1)


def section_backward(
    layer_in, out_grad, gain_row, gate_weight, value_weight, out_weight, r_local, l_local
):
    row_count, feature_width = layer_in.shape
    seq_count = lax.axis_size("seq")
    inputs_f = layer_in.astype(jnp.float32)
    inv_scale = lax.rsqrt(jnp.mean(inputs_f * inputs_f, axis=-1, keepdims=True) + epsilon)
    normed = (inputs_f * inv_scale * gain_row).astype(jnp.bfloat16)
    gate_pre = block_apply(normed, gate_weight)
    values = block_apply(normed, value_weight).astype(jnp.bfloat16)
    first_mix = jnp.dot(r_local, values, preferred_element_type=jnp.float32).astype(jnp.bfloat16)
    inner_grad = block_back(out_grad, out_weight)
    gate_sigmoid = jax.nn.sigmoid(gate_pre)
    mixed_grad = (inner_grad * gate_pre * gate_sigmoid).astype(jnp.bfloat16)
    arrived_rows = lax.all_to_all(
        first_mix.reshape(seq_count, -1, feature_width),
        "seq",
        split_axis=0,
        concat_axis=0,
        tiled=True,
    )
    mixed_there = jnp.einsum(
        "kpi,ikd->pkd", l_local, arrived_rows, preferred_element_type=jnp.float32
    ).astype(jnp.bfloat16)
    seq_mixed = lax.all_to_all(mixed_there, "seq", split_axis=0, concat_axis=0, tiled=True).reshape(
        row_count, feature_width
    )
    grad_rows = lax.all_to_all(
        mixed_grad.reshape(seq_count, -1, feature_width),
        "seq",
        split_axis=0,
        concat_axis=0,
        tiled=True,
    )
    folded_there = jnp.einsum(
        "kpi,pkd->ikd", l_local, grad_rows, preferred_element_type=jnp.float32
    ).astype(jnp.bfloat16)
    folded = lax.all_to_all(folded_there, "seq", split_axis=0, concat_axis=0, tiled=True).reshape(
        row_count, feature_width
    )
    gate_grad = (
        inner_grad
        * seq_mixed.astype(jnp.float32)
        * gate_sigmoid
        * (1.0 + gate_pre * (1.0 - gate_sigmoid))
    ).astype(jnp.bfloat16)
    value_grad = lax.dot_general(
        r_local, folded, (((0,), (0,)), ((), ())), preferred_element_type=jnp.float32
    ).astype(jnp.bfloat16)
    norm_grad = (
        block_back(gate_grad, gate_weight) + block_back(value_grad, value_weight)
    ) * gain_row
    result = (
        out_grad.astype(jnp.float32)
        + inv_scale * norm_grad
        - inv_scale
        * inv_scale
        * inv_scale
        * inputs_f
        * jnp.mean(norm_grad * inputs_f, axis=-1, keepdims=True)
    )
    return result.astype(jnp.bfloat16)


def local(
    saved_inputs, arrived_grad, loss_grad, norm_gain, w_gate, w_value, w_out, r_factor, l_factor
):
    seq_count = lax.axis_size("seq")
    l_local = l_factor[0].reshape(-1, seq_count, seq_count)
    last_section = lax.axis_index("pipe") == lax.axis_size("pipe") - 1
    incoming = arrived_grad[0]
    outputs = []
    for tick_index in range(TICKS):
        result = section_backward(
            saved_inputs[0, tick_index],
            incoming,
            norm_gain[0],
            w_gate[0],
            w_value[0],
            w_out[0],
            r_factor[0],
            l_local,
        )
        outputs.append(result)
        if tick_index + 1 < TICKS:
            passed = from_behind(result, "pipe", -1)
            incoming = jnp.where(last_section, loss_grad[tick_index], passed)
    return jnp.stack(outputs)[None]


def solution(mesh):
    placed = (
        P("pipe", None, "seq", None),
        P("pipe", "seq", None),
        P(None, "seq", None),
        P("pipe", None),
        P("pipe", None, None),
        P("pipe", None, None),
        P("pipe", None, None),
        P("pipe", "seq", None),
        P("pipe", "seq", None),
    )
    return jax.shard_map(
        local, mesh=mesh, in_specs=placed, out_specs=P("pipe", None, "seq", None), check_vma=False
    )
```

profile of v0, /device:TPU:2, one launch (start us, length us, event | category | flops | bytes accessed | tf_op | source)
XLA Modules:
  0.0 262.4 jit_solution(5766508640098185996)
XLA Ops:
  8.5 11.6 %all-to-all-start = ((bf16[32,8,1536]{2,1,0:T(8,128)(2,1)}), bf16[32,8,1536]{2,1,0:T(8,128)(2,1)}, u32[]{:S(2)}, u32[]{:S(2)}) async-start(bf16[32,8,1536]{2,1,0:T(8,128)(2,1)} %fusion.4), calls=%async_computation | async-start | bytes 1572864 | tf_op jit(solution)/shard_map/all_to_all | solution.py:52
  29.7 13.3 %all-to-all-done = bf16[32,8,1536]{2,1,0:T(8,128)(2,1)} async-done(((bf16[32,8,1536]{2,1,0:T(8,128)(2,1)}), bf16[32,8,1536]{2,1,0:T(8,128)(2,1)}, u32[]{:S(2)}, u32[]{:S(2)}) %all-to-all-start) | async-done | bytes 786464 | tf_op jit(solution)/shard_map/all_to_all | solution.py:52
  43.0 5.1 %all-to-all-start.2 = ((bf16[32,8,1536]{2,1,0:T(8,128)(2,1)}), bf16[32,8,1536]{2,1,0:T(8,128)(2,1)S(1)}, u32[]{:S(2)}, u32[]{:S(2)}) async-start(bf16[32,8,1536]{2,1,0:T(8,128)(2,1)} %reshape.293), calls=%async_computation.2 | async-start | bytes 1572864 | tf_op jit(solution)/shard_map/all_to_all | solution.py:65
  51.2 18.8 %all-to-all-done.2 = bf16[32,8,1536]{2,1,0:T(8,128)(2,1)S(1)} async-done(((bf16[32,8,1536]{2,1,0:T(8,128)(2,1)}), bf16[32,8,1536]{2,1,0:T(8,128)(2,1)S(1)}, u32[]{:S(2)}, u32[]{:S(2)}) %all-to-all-start.2) | async-done | bytes 786464 | tf_op jit(solution)/shard_map/all_to_all | solution.py:65
  70.0 5.0 %all-to-all-start.1 = ((bf16[32,8,1536]{2,1,0:T(8,128)(2,1)}), bf16[32,8,1536]{2,1,0:T(8,128)(2,1)S(1)}, u32[]{:S(2)}, u32[]{:S(2)}) async-start(bf16[32,8,1536]{2,1,0:T(8,128)(2,1)} %copy.94), calls=%async_computation.1 | async-start | bytes 1572864 | tf_op jit(solution)/shard_map/all_to_all | solution.py:62
  76.9 19.8 %all-to-all-done.1 = bf16[32,8,1536]{2,1,0:T(8,128)(2,1)S(1)} async-done(((bf16[32,8,1536]{2,1,0:T(8,128)(2,1)}), bf16[32,8,1536]{2,1,0:T(8,128)(2,1)S(1)}, u32[]{:S(2)}, u32[]{:S(2)}) %all-to-all-start.1) | async-done | bytes 786464 | tf_op jit(solution)/shard_map/all_to_all | solution.py:62
  97.5 5.1 %all-to-all-start.3 = ((bf16[32,8,1536]{2,1,0:T(8,128)(2,1)}), bf16[32,8,1536]{2,1,0:T(8,128)(2,1)}, u32[]{:S(2)}, u32[]{:S(2)}) async-start(bf16[32,8,1536]{2,1,0:T(8,128)(2,1)} %copy.104), calls=%async_computation.3 | async-start | bytes 1572864 | tf_op jit(solution)/shard_map/all_to_all | solution.py:75
  109.2 4.9 %fusion.55 = f32[4,256,384]{2,1,0:T(8,128)} fusion(f32[4,256,384]{1,2,0:T(8,128)} %get-tuple-element.12, f32[256,4,384]{0,2,1:T(8,128)} %copy.95, f32[4,384,256]{2,1,0:T(8,128)} %copy-done.15, bf16[384,4,384]{2,1,0:T(4,128)(2,1)} %reshape_squeeze.26), kind=kOutput, calls=%fused_computation.91 | convolution fusion | flops 305922048 | bytes 7471104 | tf_op jit(solution)/shard_map/rnb,cnb->rnc/dot_general | solution.py:33
  114.2 9.9 %all-to-all-done.3 = bf16[32,8,1536]{2,1,0:T(8,128)(2,1)} async-done(((bf16[32,8,1536]{2,1,0:T(8,128)(2,1)}), bf16[32,8,1536]{2,1,0:T(8,128)(2,1)}, u32[]{:S(2)}, u32[]{:S(2)}) %all-to-all-start.3) | async-done | bytes 786464 | tf_op jit(solution)/shard_map/all_to_all | solution.py:75
  125.6 3.9 %fusion.28 = (f32[256]{0:T(256)S(1)}, f32[4,256,384]{2,1,0:T(8,128)}) fusion(f32[256,4,384]{2,0,1:T(8,128)} %copy.108, f32[4,384]{1,0:T(4,128)S(1)} %mul.262, f32[4,256,384]{2,1,0:T(8,128)} %fusion.55, bf16[256,4,384]{0,2,1:T(8,128)(2,1)S(1)} %bitcast.202, bf16[384,4,384]{2,1,0:T(4,128)(2,1)S(1)} %copy-done.4), kind=kOutput, calls=%fused_computation.49 | convolution fusion | flops 303562496 | bytes 6691840 | tf_op jit(solution)/shard_map/rnb,cnb->rnc/dot_general | solution.py:33
  131.4 2.6 fusion.10
  142.4 4.9 %all-to-all-start.4 = ((bf16[32,8,1536]{2,1,0:T(8,128)(2,1)}), bf16[32,8,1536]{2,1,0:T(8,128)(2,1)}, u32[]{:S(2)}, u32[]{:S(2)}) async-start(bf16[32,8,1536]{2,1,0:T(8,128)(2,1)} %fusion.5), calls=%async_computation.4 | async-start | bytes 1572864 | tf_op jit(solution)/shard_map/all_to_all | solution.py:52
  160.4 10.2 %all-to-all-done.4 = bf16[32,8,1536]{2,1,0:T(8,128)(2,1)} async-done(((bf16[32,8,1536]{2,1,0:T(8,128)(2,1)}), bf16[32,8,1536]{2,1,0:T(8,128)(2,1)}, u32[]{:S(2)}, u32[]{:S(2)}) %all-to-all-start.4) | async-done | bytes 786464 | tf_op jit(solution)/shard_map/all_to_all | solution.py:52
  170.5 5.6 %all-to-all-start.6 = ((bf16[32,8,1536]{2,1,0:T(8,128)(2,1)}), bf16[32,8,1536]{2,1,0:T(8,128)(2,1)}, u32[]{:S(2)}, u32[]{:S(2)}) async-start(bf16[32,8,1536]{2,1,0:T(8,128)(2,1)} %reshape.294), calls=%async_computation.6 | async-start | bytes 1572864 | tf_op jit(solution)/shard_map/all_to_all | solution.py:65
  179.1 18.9 %all-to-all-done.6 = bf16[32,8,1536]{2,1,0:T(8,128)(2,1)} async-done(((bf16[32,8,1536]{2,1,0:T(8,128)(2,1)}), bf16[32,8,1536]{2,1,0:T(8,128)(2,1)}, u32[]{:S(2)}, u32[]{:S(2)}) %all-to-all-start.6) | async-done | bytes 786464 | tf_op jit(solution)/shard_map/all_to_all | solution.py:65
  198.0 5.4 %all-to-all-start.5 = ((bf16[32,8,1536]{2,1,0:T(8,128)(2,1)}), bf16[32,8,1536]{2,1,0:T(8,128)(2,1)}, u32[]{:S(2)}, u32[]{:S(2)}) async-start(bf16[32,8,1536]{2,1,0:T(8,128)(2,1)} %copy.119), calls=%async_computation.5 | async-start | bytes 1572864 | tf_op jit(solution)/shard_map/all_to_all | solution.py:62
  206.5 18.8 %all-to-all-done.5 = bf16[32,8,1536]{2,1,0:T(8,128)(2,1)} async-done(((bf16[32,8,1536]{2,1,0:T(8,128)(2,1)}), bf16[32,8,1536]{2,1,0:T(8,128)(2,1)}, u32[]{:S(2)}, u32[]{:S(2)}) %all-to-all-start.5) | async-done | bytes 786464 | tf_op jit(solution)/shard_map/all_to_all | solution.py:62
  225.3 5.1 %all-to-all-start.7 = ((bf16[32,8,1536]{2,1,0:T(8,128)(2,1)}), bf16[32,8,1536]{2,1,0:T(8,128)(2,1)}, u32[]{:S(2)}, u32[]{:S(2)}) async-start(bf16[32,8,1536]{2,1,0:T(8,128)(2,1)} %copy.129), calls=%async_computation.7 | async-start | bytes 1572864 | tf_op jit(solution)/shard_map/all_to_all | solution.py:75
  231.9 2.7 %reshape.288 = f32[256,4,384]{2,1,0:T(4,128)} reshape(bf16[32,8,1536]{2,1,0:T(8,128)(2,1)} %all-to-all-done.5) | data formatting | bytes 2359296 | tf_op jit(solution)/shard_map/convert_element_type | solution.py:80
  234.6 2.6 copy.120
  237.2 2.7 %fusion.7 = bf16[1,256,1536]{1,2,0:T(8,128)(2,1)} fusion(bf16[1,256,1536]{1,2,0:T(8,128)(2,1)} %copy.86, f32[256,4,384]{0,2,1:T(8,128)S(1)} %copy.107, bf16[1,1,256,1536]{2,3,1,0:T(8,128)(2,1)S(1)} %copy.149, f32[256]{0:T(256)S(1)} %broadcast_multiply_fusion.1, f32[256]{0:T(256)S(1)} %get-tuple-element.9, f32[1536]{0:T(1024)S(1)} %reduce.2, ...), kind=kLoop, calls=%fused_computation.17 | loop fusion | flops 3538944 | bytes 3941376 | tf_op jit(solution)/shard_map/convert_element_type | solution.py:99
  239.9 4.0 %fusion.57 = f32[4,256,384]{2,1,0:T(8,128)} fusion(f32[4,256,384]{1,2,0:T(8,128)} %get-tuple-element.16, f32[256,4,384]{0,2,1:T(8,128)S(1)} %copy-done.16, f32[4,256,384]{1,2,0:T(8,128)S(1)} %copy-done.14, bf16[384,4,384]{2,1,0:T(4,128)(2,1)} %reshape_squeeze.26), kind=kOutput, calls=%fused_computation.92 | convolution fusion | flops 305922048 | bytes 7471104 | tf_op jit(solution)/shard_map/rnb,cnb->rnc/dot_general | solution.py:33
  243.8 8.3 %all-to-all-done.7 = bf16[32,8,1536]{2,1,0:T(8,128)(2,1)} async-done(((bf16[32,8,1536]{2,1,0:T(8,128)(2,1)}), bf16[32,8,1536]{2,1,0:T(8,128)(2,1)}, u32[]{:S(2)}, u32[]{:S(2)}) %all-to-all-start.7) | async-done | bytes 786464 | tf_op jit(solution)/shard_map/all_to_all | solution.py:75
  253.7 3.8 %fusion.11 = (f32[256]{0:T(256)S(1)}, f32[4,256,384]{2,1,0:T(8,128)}) fusion(f32[256,4,384]{2,0,1:T(8,128)} %copy.133, f32[4,384]{1,0:T(4,128)S(1)} %mul.262, f32[4,256,384]{2,1,0:T(8,128)} %fusion.57, bf16[256,4,384]{0,2,1:T(8,128)(2,1)S(1)} %bitcast.201, bf16[384,4,384]{2,1,0:T(4,128)(2,1)S(1)} %copy-done.6), kind=kOutput, calls=%fused_computation.23 | convolution fusion | flops 303562496 | bytes 6691840 | tf_op jit(solution)/shard_map/rnb,cnb->rnc/dot_general | solution.py:33
  (102 shorter events, 68.8 us)
Async XLA Ops:
  0.0 7.2 %copy-start = (bf16[1,256,256]{2,1,0:T(8,128)(2,1)S(1)}, bf16[1,256,256]{2,1,0:T(8,128)(2,1)}, u32[]{:S(2)}) copy-start(bf16[1,256,256]{2,1,0:T(8,128)(2,1)} %param.16) | copy-start | bytes 393220
  4.0 1.8 copy-start.3
  7.2 12.9 %copy-start.18 = (bf16[1,384,1536]{2,1,0:T(8,128)(2,1)S(1)}, bf16[1,384,1536]{2,1,0:T(8,128)(2,1)}, u32[]{:S(2)}) copy-start(bf16[1,384,1536]{2,1,0:T(8,128)(2,1)} %param.13) | copy-start | bytes 3538948
  8.5 34.5 %all-to-all-start = ((bf16[32,8,1536]{2,1,0:T(8,128)(2,1)}), bf16[32,8,1536]{2,1,0:T(8,128)(2,1)}, u32[]{:S(2)}, u32[]{:S(2)}) async-start(bf16[32,8,1536]{2,1,0:T(8,128)(2,1)} %fusion.4), calls=%async_computation | async-start | bytes 1572864 | tf_op jit(solution)/shard_map/all_to_all | solution.py:52
  22.1 2.8 %copy-start.1 = (bf16[384,4,384]{2,1,0:T(4,128)(2,1)}, bf16[384,4,384]{2,1,0:T(4,128)(2,1)S(1)}, u32[]{:S(2)}) copy-start(bf16[384,4,384]{2,1,0:T(4,128)(2,1)S(1)} %reshape_squeeze.10) | copy-start | bytes 3538948
  25.6 2.2 copy-start.15
  28.5 19.7 %copy-start.22 = (bf16[1,8,1024]{2,1,0:T(8,128)(2,1)S(1)}, bf16[1,8,1024]{2,1,0:T(8,128)(2,1)}, u32[]{:S(2)}) copy-start(bf16[1,8,1024]{2,1,0:T(8,128)(2,1)} %param.17) | copy-start | bytes 49156
  43.0 27.0 %all-to-all-start.2 = ((bf16[32,8,1536]{2,1,0:T(8,128)(2,1)}), bf16[32,8,1536]{2,1,0:T(8,128)(2,1)S(1)}, u32[]{:S(2)}, u32[]{:S(2)}) async-start(bf16[32,8,1536]{2,1,0:T(8,128)(2,1)} %reshape.293), calls=%async_computation.2 | async-start | bytes 1572864 | tf_op jit(solution)/shard_map/all_to_all | solution.py:65
  70.0 26.7 %all-to-all-start.1 = ((bf16[32,8,1536]{2,1,0:T(8,128)(2,1)}), bf16[32,8,1536]{2,1,0:T(8,128)(2,1)S(1)}, u32[]{:S(2)}, u32[]{:S(2)}) async-start(bf16[32,8,1536]{2,1,0:T(8,128)(2,1)} %copy.94), calls=%async_computation.1 | async-start | bytes 1572864 | tf_op jit(solution)/shard_map/all_to_all | solution.py:62
  97.5 26.5 %all-to-all-start.3 = ((bf16[32,8,1536]{2,1,0:T(8,128)(2,1)}), bf16[32,8,1536]{2,1,0:T(8,128)(2,1)}, u32[]{:S(2)}, u32[]{:S(2)}) async-start(bf16[32,8,1536]{2,1,0:T(8,128)(2,1)} %copy.104), calls=%async_computation.3 | async-start | bytes 1572864 | tf_op jit(solution)/shard_map/all_to_all | solution.py:75
  102.7 2.6 copy-start.10
  114.2 11.4 %copy-start.4 = (bf16[384,4,384]{2,1,0:T(4,128)(2,1)S(1)}, bf16[384,4,384]{2,1,0:T(4,128)(2,1)}, u32[]{:S(2)}) copy-start(bf16[384,4,384]{2,1,0:T(4,128)(2,1)} %copy-done.3) | copy-start | bytes 3538948
  131.3 4.5 %copy-start.5 = (bf16[384,4,384]{2,1,0:T(4,128)(2,1)S(1)}, bf16[384,4,384]{2,1,0:T(4,128)(2,1)}, u32[]{:S(2)}) copy-start(bf16[384,4,384]{2,1,0:T(4,128)(2,1)} %copy-done.3) | copy-start | bytes 3538948
  133.9 15.8 %collective-permute-start = (bf16[256,1536]{0,1:T(8,128)(2,1)}, bf16[256,1536]{0,1:T(8,128)(2,1)}, u32[]{:S(2)}, u32[]{:S(2)}) collective-permute-start(bf16[256,1536]{0,1:T(8,128)(2,1)} %fusion.10), channel_id=1, source_target_pairs={{32,0},{64,32},{96,64},{128,96},{160,128},{192,160},{224,192},{33,... | collective-permute-start | bytes 2359304 | tf_op jit(solution)/shard_map/ppermute | solution.py:15
  142.4 28.1 %all-to-all-start.4 = ((bf16[32,8,1536]{2,1,0:T(8,128)(2,1)}), bf16[32,8,1536]{2,1,0:T(8,128)(2,1)}, u32[]{:S(2)}, u32[]{:S(2)}) async-start(bf16[32,8,1536]{2,1,0:T(8,128)(2,1)} %fusion.5), calls=%async_computation.4 | async-start | bytes 1572864 | tf_op jit(solution)/shard_map/all_to_all | solution.py:52
  149.7 2.5 copy-start.2
  153.4 2.4 copy-start.13
  170.5 27.5 %all-to-all-start.6 = ((bf16[32,8,1536]{2,1,0:T(8,128)(2,1)}), bf16[32,8,1536]{2,1,0:T(8,128)(2,1)}, u32[]{:S(2)}, u32[]{:S(2)}) async-start(bf16[32,8,1536]{2,1,0:T(8,128)(2,1)} %reshape.294), calls=%async_computation.6 | async-start | bytes 1572864 | tf_op jit(solution)/shard_map/all_to_all | solution.py:65
  198.0 27.3 %all-to-all-start.5 = ((bf16[32,8,1536]{2,1,0:T(8,128)(2,1)}), bf16[32,8,1536]{2,1,0:T(8,128)(2,1)}, u32[]{:S(2)}, u32[]{:S(2)}) async-start(bf16[32,8,1536]{2,1,0:T(8,128)(2,1)} %copy.119), calls=%async_computation.5 | async-start | bytes 1572864 | tf_op jit(solution)/shard_map/all_to_all | solution.py:62
  225.3 26.8 %all-to-all-start.7 = ((bf16[32,8,1536]{2,1,0:T(8,128)(2,1)}), bf16[32,8,1536]{2,1,0:T(8,128)(2,1)}, u32[]{:S(2)}, u32[]{:S(2)}) async-start(bf16[32,8,1536]{2,1,0:T(8,128)(2,1)} %copy.129), calls=%async_computation.7 | async-start | bytes 1572864 | tf_op jit(solution)/shard_map/all_to_all | solution.py:75
  237.2 2.7 %copy-start.14 = (f32[4,256,384]{1,2,0:T(8,128)S(1)}, f32[4,256,384]{1,2,0:T(8,128)}, u32[]{:S(2)}) copy-start(f32[4,256,384]{1,2,0:T(8,128)} %copy-done.13) | copy-start | bytes 4718596
  237.2 2.7 %copy-start.16 = (f32[256,4,384]{0,2,1:T(8,128)S(1)}, f32[256,4,384]{0,2,1:T(8,128)}, u32[]{:S(2)}) copy-start(f32[256,4,384]{0,2,1:T(8,128)} %copy.120) | copy-start | bytes 4718596
  243.8 9.8 %copy-start.6 = (bf16[384,4,384]{2,1,0:T(4,128)(2,1)S(1)}, bf16[384,4,384]{2,1,0:T(4,128)(2,1)}, u32[]{:S(2)}) copy-start(bf16[384,4,384]{2,1,0:T(4,128)(2,1)} %copy-done.3) | copy-start | bytes 3538948
  257.5 2.0 copy-start.8
  (9 other events, 10.6 us)
where the time goes:
time: 266 us; the launch traced here: 262 us
  waiting for transfers between devices  118 us (44%)
  starting transfers between devices  49.9 us (19%)
  local copies, waits for them, and re-layouts  48 us (18%)
  matrix products  38.2 us (14%)
  other arithmetic  7.91 us (3%)
    all_to_all x2, waiting for transfers between devices, section_backward(): lax.all_to_all(mixed_there, 'seq', split_axis=0, concat_axis=0, tiled=True)  38.6 us
    all_to_all x2, waiting for transfers between devices, section_backward(): lax.all_to_all(mixed_grad.reshape(seq_count, -1, feature_width), 'seq', s...  37.7 us
    all_to_all x2, waiting for transfers between devices, section_backward(): lax.all_to_all(first_mix.reshape(seq_count, -1, feature_width), 'seq', sp...  23.5 us
    all_to_all x2, waiting for transfers between devices, section_backward(): lax.all_to_all(folded_there, 'seq', split_axis=0, concat_axis=0, tiled=True)  18.1 us
    dot_general x6, matrix products, block_back(): jnp.einsum('rnb,cnb->rnc', left_blocks, right_blocks, preferred_element_t...  17.8 us
    all_to_all x2, starting transfers between devices, section_backward(): lax.all_to_all(first_mix.reshape(seq_count, -1, feature_width), 'seq', sp...  16.5 us
    all_to_all x2, starting transfers between devices, section_backward(): lax.all_to_all(mixed_grad.reshape(seq_count, -1, feature_width), 'seq', s...  10.7 us
    all_to_all x2, starting transfers between devices, section_backward(): lax.all_to_all(mixed_there, 'seq', split_axis=0, concat_axis=0, tiled=True)  10.5 us
  transfers between devices with their start and end apart: 9, of which 8 were waited for; matrix products, arithmetic and copies ran while one was open for 24% of the time, Pallas kernels for 0%

commit v1 on v0

v1 whole, which is shorter than its diff:
```python
import functools

import jax
import jax.numpy as jnp
from jax import lax
from jax.experimental import pallas as pl
from jax.experimental.pallas import tpu as pltpu
from jax.sharding import PartitionSpec as P

TICKS = 2
NBLK = 4
MESH = pl.DeviceIdType.MESH
F32 = jnp.float32
BF16 = jnp.bfloat16

epsilon = 1e-05

A0, G0, M0, V0, A1, G1, M1, V1 = range(8)


def dot_nn(a, b):
    return lax.dot_general(a, b, (((1,), (0,)), ((), ())), preferred_element_type=F32)


def dot_nt(a, b):
    return lax.dot_general(a, b, (((1,), (1,)), ((), ())), preferred_element_type=F32)


def kernel(
    x_h, dy_h, lg_h, gain_h, wg_h, wv_h, wo_h, r_h, l_h, out_h,
    x_v, dy_v, lg_v, gain_v, wg_v, wv_v, wo_v, r_v, rt_v, l_v, lb_v, lbt_v,
    src, dst, coef, silu, slope, e_v, q_v, acc, res, dyn,
    load_sem, out_sem, send_sem, recv_sem, psend, precv,
):
    nseq = lax.axis_size("seq")
    npipe = lax.axis_size("pipe")
    me = lax.axis_index("seq")
    pi = lax.axis_index("pipe")
    before = lax.rem(pi + npipe - 1, npipe)
    after = lax.rem(pi + 1, npipe)
    width = wg_v.shape[0]
    rows = r_v.shape[0]
    per = rows // nseq
    model = gain_v.shape[1]

    pairs = (
        (x_h.at[0, 0], x_v.at[0]),
        (wv_h.at[0], wv_v),
        (r_h.at[0], r_v),
        (gain_h, gain_v),
        (wg_h.at[0], wg_v),
        (wo_h.at[0], wo_v),
        (dy_h.at[0], dy_v),
        (l_h.at[0], l_v),
        (x_h.at[0, 1], x_v.at[1]),
        (lg_h.at[0], lg_v),
    )
    loads = [pltpu.make_async_copy(a, b, load_sem.at[i]) for i, (a, b) in enumerate(pairs)]
    for c in loads:
        c.start()

    barrier = pltpu.get_barrier_semaphore()

    def greet(j, carry):
        pl.semaphore_signal(
            barrier, inc=1, device_id={"seq": lax.rem(me + j, nseq)}, device_id_type=MESH
        )
        return carry

    lax.fori_loop(1, nseq, greet, 0)
    for other in (before, after):
        pl.semaphore_signal(barrier, inc=1, device_id={"pipe": other}, device_id_type=MESH)

    def copy_to(a, n, peer):
        return pltpu.make_async_remote_copy(
            src_ref=src.at[a, n, peer],
            dst_ref=dst.at[a, n, me],
            send_sem=send_sem.at[a, n],
            recv_sem=recv_sem.at[a, n],
            device_id={"seq": peer},
            device_id_type=MESH,
        )

    def send(a, n):
        def body(j, carry):
            copy_to(a, n, lax.rem(me + j, nseq)).start()
            copy_to(a, n, lax.rem(me + nseq - j, nseq)).start()
            return carry

        lax.fori_loop(1, nseq // 2, body, 0)
        copy_to(a, n, lax.rem(me + nseq // 2, nseq)).start()
        dst[a, n, me] = src[a, n, me]

    def whole(a, n):
        return pltpu.make_async_remote_copy(
            src_ref=src.at[a, n, pl.ds(0, nseq - 1)],
            dst_ref=dst.at[a, n, pl.ds(0, nseq - 1)],
            send_sem=send_sem.at[a, n],
            recv_sem=recv_sem.at[a, n],
            device_id={"seq": lax.rem(me + 1, nseq)},
            device_id_type=MESH,
        )

    def put(a, n, value):
        src[a, n] = value.reshape(nseq, per, width).astype(BF16)

    def take(a, n):
        return dst[a, n].astype(F32).reshape(rows, width)

    def cols(n):
        return pl.ds(pl.multiple_of(n * width, 128), width)

    def each(body):
        def step(n, carry):
            body(n)
            return carry

        lax.fori_loop(0, NBLK, step, 0)

    def scale_of(t):
        total = jnp.zeros((rows, 1), F32)
        for n in range(NBLK):
            v = x_v[t, :, n * width : (n + 1) * width].astype(F32)
            total = total + jnp.sum(v * v, axis=-1, keepdims=True)
        q_v[t] = lax.rsqrt(total * (1.0 / model) + epsilon)

    def normed_of(t, n):
        return (x_v[t, :, cols(n)].astype(F32) * q_v[t] * gain_v[:, cols(n)]).astype(BF16)

    for i in range(4):
        loads[i].wait()
    scale_of(0)

    def front0(n):
        normed = normed_of(0, n)
        values = dot_nn(normed, wv_v[:, cols(n)]).astype(BF16)
        put(A0, n, dot_nn(r_v[...], values))

    def back0(n):
        normed = normed_of(0, n)
        gate = dot_nn(normed, wg_v[:, cols(n)])
        inner = dot_nt(dy_v[:, cols(n)], wo_v[:, cols(n)])
        sig = jax.nn.sigmoid(gate)
        put(G0, n, inner * gate * sig)
        coef[n] = inner * (sig * (1.0 + gate * (1.0 - sig)))

    front0(0)
    pl.semaphore_wait(barrier, nseq + 1)
    send(A0, 0)
    for i in range(4, 7):
        loads[i].wait()

    def start0(n):
        @pl.when(n > 0)
        def _():
            front0(n)
            send(A0, n)

        back0(n)
        send(G0, n)

    each(start0)

    loads[7].wait()
    rt_v[...] = r_v[...].astype(F32).T.astype(BF16)
    wide = l_v.shape[1]
    tiled = jnp.broadcast_to(l_v[...].astype(F32)[None], (nseq, per, wide)).reshape(rows, wide)
    row = lax.broadcasted_iota(jnp.int32, (rows, wide), 0)
    col = lax.broadcasted_iota(jnp.int32, (rows, wide), 1)
    own = jnp.where(col // nseq == row // per, tiled, 0.0).astype(BF16)
    col_c = lax.broadcasted_iota(jnp.int32, (wide, rows), 0)
    row_c = lax.broadcasted_iota(jnp.int32, (wide, rows), 1)
    spread = jnp.where(col_c % nseq == row_c // per, 1.0, 0.0).astype(BF16)
    big = dot_nn(own, spread)
    ra = lax.broadcasted_iota(jnp.int32, (rows, rows), 0)
    rb = lax.broadcasted_iota(jnp.int32, (rows, rows), 1)
    big = jnp.where(ra % per == rb % per, big, 0.0)
    lb_v[...] = big.astype(BF16)
    lbt_v[...] = big.T.astype(BF16)

    loads[8].wait()
    scale_of(1)

    def front1(n):
        normed = normed_of(1, n)
        values = dot_nn(normed, wv_v[:, cols(n)]).astype(BF16)
        put(A1, n, dot_nn(r_v[...], values))
        gate = dot_nn(normed, wg_v[:, cols(n)])
        sig = jax.nn.sigmoid(gate)
        silu[n] = gate * sig
        slope[n] = sig * (1.0 + gate * (1.0 - sig))

    each(front1)

    def mix(a, b, n):
        whole(a, n).wait_recv()
        put(b, n, dot_nn(lb_v[...], take(a, n).astype(BF16)))
        send(b, n)

    def fold(a, b, n):
        whole(a, n).wait_recv()
        put(b, n, dot_nn(lbt_v[...], take(a, n).astype(BF16)))
        send(b, n)

    def turn0(n):
        mix(A0, M0, n)
        fold(G0, V0, n)

    each(turn0)
    each(functools.partial(send, A1))

    def finish(t, m, v):
        acc[...] = jnp.zeros_like(acc)

        def part(n):
            whole(m, n).wait_recv()
            gate_grad = (coef[n] * take(m, n)).astype(BF16)
            left = dot_nt(gate_grad, wg_v[:, cols(n)])
            whole(v, n).wait_recv()
            value_grad = dot_nn(rt_v[...], take(v, n).astype(BF16)).astype(BF16)
            e = (left + dot_nt(value_grad, wv_v[:, cols(n)])) * gain_v[:, cols(n)]
            e_v[n] = e
            acc[...] += jnp.sum(e * x_v[t, :, cols(n)].astype(F32), axis=-1, keepdims=True)

        each(part)

    def result(t, n, dy):
        q = q_v[t]
        mean = acc[...] * (1.0 / model)
        value = dy.astype(F32) + q * e_v[n] - (q * q * q * mean) * x_v[t, :, cols(n)].astype(F32)
        res[t, n] = value.astype(BF16)

    def write(t, n):
        return pltpu.make_async_copy(res.at[t, n], out_h.at[0, t, :, cols(n)], out_sem.at[t, n])

    def passing(n):
        return pltpu.make_async_remote_copy(
            src_ref=res.at[0, n],
            dst_ref=dyn.at[n],
            send_sem=psend.at[n],
            recv_sem=precv.at[n],
            device_id={"pipe": before},
            device_id_type=MESH,
        )

    finish(0, M0, V0)

    def hand_on(n):
        result(0, n, dy_v[:, cols(n)])
        passing(n).start()
        write(0, n).start()

    each(hand_on)

    loads[9].wait()
    last = pi == npipe - 1

    def start1(n):
        passing(n).wait_recv()
        dy = jnp.where(last, lg_v[:, cols(n)].astype(F32), dyn[n].astype(F32)).astype(BF16)
        dy_v[:, cols(n)] = dy
        inner = dot_nt(dy, wo_v[:, cols(n)])
        put(G1, n, inner * silu[n])
        coef[n] = inner * slope[n]
        send(G1, n)
        mix(A1, M1, n)

    each(start1)
    each(functools.partial(fold, G1, V1))
    finish(1, M1, V1)

    def end(n):
        result(1, n, dy_v[:, cols(n)])
        write(1, n).start()

    each(end)

    def drain(n):
        for a in range(8):
            whole(a, n).wait_send()
        passing(n).wait_send()
        write(0, n).wait()
        write(1, n).wait()

    each(drain)


def local(*args):
    saved, _, _, _, w_gate, _, _, r_factor, l_factor = args
    _, ticks, rows, model = saved.shape
    width = w_gate.shape[1]
    nseq = lax.axis_size("seq")
    per = rows // nseq
    anywhere = pl.BlockSpec(memory_space=pl.ANY)
    vmem = pltpu.VMEM
    dma = pltpu.SemaphoreType.DMA
    return pl.pallas_call(
        kernel,
        out_shape=jax.ShapeDtypeStruct(saved.shape, BF16),
        in_specs=[anywhere] * len(args),
        out_specs=anywhere,
        scratch_shapes=[
            vmem((ticks, rows, model), BF16),
            vmem((rows, model), BF16),
            vmem((rows, model), BF16),
            vmem((1, model), F32),
            vmem((width, model), BF16),
            vmem((width, model), BF16),
            vmem((width, model), BF16),
            vmem((rows, rows), BF16),
            vmem((rows, rows), BF16),
            vmem(l_factor.shape[1:], BF16),
            vmem((rows, rows), BF16),
            vmem((rows, rows), BF16),
            vmem((8, NBLK, nseq, per, width), BF16),
            vmem((8, NBLK, nseq, per, width), BF16),
            vmem((NBLK, rows, width), F32),
            vmem((NBLK, rows, width), F32),
            vmem((NBLK, rows, width), F32),
            vmem((NBLK, rows, width), F32),
            vmem((ticks, rows, 1), F32),
            vmem((rows, 1), F32),
            vmem((ticks, NBLK, rows, width), BF16),
            vmem((NBLK, rows, width), BF16),
            dma((10,)),
            dma((ticks, NBLK)),
            dma((8, NBLK)),
            dma((8, NBLK)),
            dma((NBLK,)),
            dma((NBLK,)),
        ],
        compiler_params=pltpu.CompilerParams(
            collective_id=0, has_side_effects=True, vmem_limit_bytes=60 * 2**20
        ),
    )(*args)


def solution(mesh):
    placed = (
        P("pipe", None, "seq", None),
        P("pipe", "seq", None),
        P(None, "seq", None),
        P("pipe", None),
        P("pipe", None, None),
        P("pipe", None, None),
        P("pipe", None, None),
        P("pipe", "seq", None),
        P("pipe", "seq", None),
    )
    return jax.shard_map(
        local, mesh=mesh, in_specs=placed, out_specs=P("pipe", None, "seq", None), check_vma=False
    )
```

time: 266 us -> 153 us (0.58); the launches traced: 262 us -> 153 us
  Pallas kernels: 0 us -> 150 us
  waiting for transfers between devices: 118 us -> 0 us
  starting transfers between devices: 49.9 us -> 0 us
  local copies, waits for them, and re-layouts: 48 us -> 2.65 us
  matrix products: 38.2 us -> 0 us
  other arithmetic: 7.91 us -> 0 us
    pallas_call x0 -> x1, Pallas kernels: none -> 150 us  [local(): pl.pallas_call(kernel, out_shape=jax.ShapeDtypeStruct(saved.shape, BF16),...]
    all_to_all x8 -> x0, waiting for transfers between devices: 118 us -> none  [the longest x2 38.6 us: section_backward(): lax.all_to_all(mixed_there, 'seq', split_axis=0, concat_axis=0, tiled=True)]
    all_to_all x8 -> x0, starting transfers between devices: 48 us -> none  [the longest x2 16.5 us: section_backward(): lax.all_to_all(first_mix.reshape(seq_count, -1, feature_width), 'seq', sp...]
    dot_general x18 -> x0, matrix products: 38.2 us -> none  [the longest x6 17.8 us: block_back(): jnp.einsum('rnb,cnb->rnc', left_blocks, right_blocks, preferred_element_t...]
    convert_element_type x16 -> x0, local copies, waits for them, and re-layouts: 27 us -> none  [the longest x4 8.75 us: section_backward(): seq_mixed.astype(jnp.float32)]
    unnamed x52 -> x1, local copies, waits for them, and re-layouts: 9.03 us -> 2.65 us
    convert_element_type x3 -> x0, other arithmetic: 5.69 us -> none  [section_backward(): return result.astype(jnp.bfloat16)]
    another operation x5 -> x0, local copies, waits for them, and re-layouts: 4.11 us -> none  [the longest x1 2.16 us: block_back(): left_blocks = rows_in.reshape(row_count, -1, block_width)]
  transfers between devices with their start and end apart: 9 -> 0, of which waited for: 8 -> 0; matrix products, arithmetic and copies ran while one was open for 24% -> 0% of each run, Pallas kernels for 0% -> 0%
where the time goes in v1:
time: 153 us
  Pallas kernels  150 us (98%)
  local copies, waits for them, and re-layouts  2.65 us (2%)
    pallas_call x1, Pallas kernels, local(): pl.pallas_call(kernel, out_shape=jax.ShapeDtypeStruct(saved.shape, BF16),...  150 us

profile of v1, /device:TPU:2, one launch (start us, length us, event | category | flops | bytes accessed | tf_op | source)
XLA Modules:
  0.0 152.7 jit_solution(17382410298141171697)
XLA Ops:
  0.0 150.1 %shard_map.91 = bf16[1,2,256,1536]{3,2,1,0:T(8,128)(2,1)} custom-call(bf16[1,2,256,1536]{3,2,1,0:T(8,128)(2,1)} %x_h.1, bf16[1,256,1536]{2,1,0:T(8,128)(2,1)} %dy_h.1, bf16[1,256,1536]{2,1,0:T(8,128)(2,1)} %lg_h.1, f32[1,1536]{1,0:T(1,128)} %gain_h.1, bf16[1,384,1536]{2,1,0:T(8,128)(2,1)} %wg_h.1, bf16[1,384,1536]{2,1,0:T(8,128)(2,1)} %wv_h.1, ...), custom_call_target="tpu_custom_call" | custom-call | tf_op jit(solution)/shard_map/pallas_call | solution.py:297
  150.1 2.7 %copy.11 = bf16[1,2,256,1536]{3,2,1,0:T(8,128)(2,1)} copy(bf16[1,2,256,1536]{3,2,1,0:T(8,128)(2,1)} %shard_map.91) | data formatting | bytes 3145728

commit v2 on v1

--- a/solution.py
+++ b/solution.py
@@ -27,10 +27,11 @@
 
 
 def kernel(
-    x_h, dy_h, lg_h, gain_h, wg_h, wv_h, wo_h, r_h, l_h, out_h,
-    x_v, dy_v, lg_v, gain_v, wg_v, wv_v, wo_v, r_v, rt_v, l_v, lb_v, lbt_v,
-    src, dst, coef, silu, slope, e_v, q_v, acc, res, dyn,
-    load_sem, out_sem, send_sem, recv_sem, psend, precv,
+    x_h, dy_h, lg_h, gain_h, wg_h, wv_h, wo_h, r_h, l_h,
+    out0, x1_v, base, weight,
+    x0_v, dy_v, lg_v, gain_v, wg_v, wv_v, wo_v, r_v, rt_v, l_v, lb_v, lbt_v,
+    src, dst, coef, silu, slope, q_v, acc, res, dyn,
+    load_sem, send_sem, recv_sem, psend, precv,
 ):
     nseq = lax.axis_size("seq")
     npipe = lax.axis_size("pipe")
@@ -43,8 +44,9 @@
     per = rows // nseq
     model = gain_v.shape[1]
 
+    x_v = (x0_v, x1_v)
     pairs = (
-        (x_h.at[0, 0], x_v.at[0]),
+        (x_h.at[0, 0], x0_v),
         (wv_h.at[0], wv_v),
         (r_h.at[0], r_v),
         (gain_h, gain_v),
@@ -52,7 +54,7 @@
         (wo_h.at[0], wo_v),
         (dy_h.at[0], dy_v),
         (l_h.at[0], l_v),
-        (x_h.at[0, 1], x_v.at[1]),
+        (x_h.at[0, 1], x1_v),
         (lg_h.at[0], lg_v),
     )
     loads = [pltpu.make_async_copy(a, b, load_sem.at[i]) for i, (a, b) in enumerate(pairs)]
@@ -120,12 +122,12 @@
     def scale_of(t):
         total = jnp.zeros((rows, 1), F32)
         for n in range(NBLK):
-            v = x_v[t, :, n * width : (n + 1) * width].astype(F32)
+            v = x_v[t][:, n * width : (n + 1) * width].astype(F32)
             total = total + jnp.sum(v * v, axis=-1, keepdims=True)
         q_v[t] = lax.rsqrt(total * (1.0 / model) + epsilon)
 
     def normed_of(t, n):
-        return (x_v[t, :, cols(n)].astype(F32) * q_v[t] * gain_v[:, cols(n)]).astype(BF16)
+        return (x_v[t][:, cols(n)].astype(F32) * q_v[t] * gain_v[:, cols(n)]).astype(BF16)
 
     for i in range(4):
         loads[i].wait()
@@ -219,23 +221,16 @@
             whole(v, n).wait_recv()
             value_grad = dot_nn(rt_v[...], take(v, n).astype(BF16)).astype(BF16)
             e = (left + dot_nt(value_grad, wv_v[:, cols(n)])) * gain_v[:, cols(n)]
-            e_v[n] = e
-            acc[...] += jnp.sum(e * x_v[t, :, cols(n)].astype(F32), axis=-1, keepdims=True)
+            base[n] = dy_v[:, cols(n)].astype(F32) + q_v[t] * e
+            acc[...] += jnp.sum(e * x_v[t][:, cols(n)].astype(F32), axis=-1, keepdims=True)
 
         each(part)
-
-    def result(t, n, dy):
         q = q_v[t]
-        mean = acc[...] * (1.0 / model)
-        value = dy.astype(F32) + q * e_v[n] - (q * q * q * mean) * x_v[t, :, cols(n)].astype(F32)
-        res[t, n] = value.astype(BF16)
-
-    def write(t, n):
-        return pltpu.make_async_copy(res.at[t, n], out_h.at[0, t, :, cols(n)], out_sem.at[t, n])
+        acc[...] = q * q * q * (acc[...] * (1.0 / model))
 
     def passing(n):
         return pltpu.make_async_remote_copy(
-            src_ref=res.at[0, n],
+            src_ref=res.at[n],
             dst_ref=dyn.at[n],
             send_sem=psend.at[n],
             recv_sem=precv.at[n],
@@ -246,9 +241,10 @@
     finish(0, M0, V0)
 
     def hand_on(n):
-        result(0, n, dy_v[:, cols(n)])
+        value = (base[n] - acc[...] * x0_v[:, cols(n)].astype(F32)).astype(BF16)
+        res[n] = value
         passing(n).start()
-        write(0, n).start()
+        out0[:, cols(n)] = value
 
     each(hand_on)
 
@@ -267,22 +263,32 @@
 
     each(start1)
     each(functools.partial(fold, G1, V1))
+
+    def drain(a, n):
+        whole(a, n).wait_send()
+
+    for a in range(7):
+        each(functools.partial(drain, a))
+    each(lambda n: passing(n).wait_send())
     finish(1, M1, V1)
-
-    def end(n):
-        result(1, n, dy_v[:, cols(n)])
-        write(1, n).start()
-
-    each(end)
-
-    def drain(n):
-        for a in range(8):
-            whole(a, n).wait_send()
-        passing(n).wait_send()
-        write(0, n).wait()
-        write(1, n).wait()
-
-    each(drain)
+    weight[...] = jnp.broadcast_to(acc[...], weight.shape)
+    each(functools.partial(drain, V1))
+
+
+def closing(out0, x1_v, base, weight, out_h, res, out_sem):
+    width = base.shape[2]
+    first = pltpu.make_async_copy(out0, out_h.at[0, 0], out_sem.at[NBLK])
+    first.start()
+    copies = []
+    for n in range(NBLK):
+        span = pl.ds(n * width, width)
+        value = base[n] - weight[:, :1] * x1_v[:, span].astype(F32)
+        res[n] = value.astype(BF16)
+        copies.append(pltpu.make_async_copy(res.at[n], out_h.at[0, 1, :, span], out_sem.at[n]))
+        copies[-1].start()
+    for c in copies:
+        c.wait()
+    first.wait()
 
 
 def local(*args):
@@ -294,13 +300,18 @@
     anywhere = pl.BlockSpec(memory_space=pl.ANY)
     vmem = pltpu.VMEM
     dma = pltpu.SemaphoreType.DMA
-    return pl.pallas_call(
+    parts = pl.pallas_call(
         kernel,
-        out_shape=jax.ShapeDtypeStruct(saved.shape, BF16),
+        out_shape=(
+            vmem((rows, model), BF16),
+            vmem((rows, model), BF16),
+            vmem((NBLK, rows, width), F32),
+            vmem((rows, 128), F32),
+        ),
         in_specs=[anywhere] * len(args),
-        out_specs=anywhere,
+        out_specs=(pl.BlockSpec(memory_space=vmem),) * 4,
         scratch_shapes=[
-            vmem((ticks, rows, model), BF16),
+            vmem((rows, model), BF16),
             vmem((rows, model), BF16),
             vmem((rows, model), BF16),
             vmem((1, model), F32),
@@ -317,13 +328,11 @@
             vmem((NBLK, rows, width), F32),
             vmem((NBLK, rows, width), F32),
             vmem((NBLK, rows, width), F32),
-            vmem((NBLK, rows, width), F32),
             vmem((ticks, rows, 1), F32),
             vmem((rows, 1), F32),
-            vmem((ticks, NBLK, rows, width), BF16),
+            vmem((NBLK, rows, width), BF16),
             vmem((NBLK, rows, width), BF16),
             dma((10,)),
-            dma((ticks, NBLK)),
             dma((8, NBLK)),
             dma((8, NBLK)),
             dma((NBLK,)),
@@ -333,6 +342,14 @@
             collective_id=0, has_side_effects=True, vmem_limit_bytes=60 * 2**20
         ),
     )(*args)
+    return pl.pallas_call(
+        closing,
+        out_shape=jax.ShapeDtypeStruct(saved.shape, BF16),
+        in_specs=[pl.BlockSpec(memory_space=vmem)] * 4,
+        out_specs=anywhere,
+        scratch_shapes=[vmem((NBLK, rows, width), BF16), dma((NBLK + 1,))],
+        compiler_params=pltpu.CompilerParams(vmem_limit_bytes=16 * 2**20),
+    )(*parts)
 
 
 def solution(mesh):

time: 153 us -> 150 us (0.980)
  local copies, waits for them, and re-layouts: 2.65 us -> 0 us
    unnamed x1 -> x0, local copies, waits for them, and re-layouts: 2.65 us -> none
    pallas_call x1 -> x2, Pallas kernels: 150 us -> 150 us  [the longest x1 149 us: local(): pl.pallas_call(kernel, out_shape=(vmem((rows, model), BF16), vmem((rows,...]
where the time goes in v2:
time: 150 us
  Pallas kernels  150 us (100%)
    pallas_call x1, Pallas kernels, local(): pl.pallas_call(kernel, out_shape=(vmem((rows, model), BF16), vmem((rows,...  149 us

profile of v2, /device:TPU:2, one launch (start us, length us, event | category | flops | bytes accessed | tf_op | source)
XLA Modules:
  0.0 149.9 jit_solution(6534864167234936623)
XLA Ops:
  0.0 148.7 %shard_map.91 = (bf16[256,1536]{1,0:T(8,128)(2,1)S(1)}, bf16[256,1536]{1,0:T(8,128)(2,1)S(1)}, f32[4,256,384]{2,1,0:T(8,128)S(1)}, f32[256,128]{1,0:T(8,128)S(1)}) custom-call(bf16[1,2,256,1536]{3,2,1,0:T(8,128)(2,1)} %x_h.1, bf16[1,256,1536]{2,1,0:T(8,128)(2,1)} %dy_h.1, bf16[1,256,1536]{2,1,0:T(8,128)(2,1)} %lg_h.1, f32[1,1536]{1,0:T(1,128)} %gain_h.1, ...), custom_call_target="tpu_custom_call" | custom-call | tf_op jit(solution)/shard_map/pallas_call | solution.py:303
  148.8 1.2 shard_map.92

commit v3 on v2

--- a/solution.py
+++ b/solution.py
@@ -9,6 +9,7 @@
 
 TICKS = 2
 NBLK = 4
+HELD = 2
 MESH = pl.DeviceIdType.MESH
 F32 = jnp.float32
 BF16 = jnp.bfloat16
@@ -30,7 +31,7 @@
     x_h, dy_h, lg_h, gain_h, wg_h, wv_h, wo_h, r_h, l_h,
     out0, x1_v, base, weight,
     x0_v, dy_v, lg_v, gain_v, wg_v, wv_v, wo_v, r_v, rt_v, l_v, lb_v, lbt_v,
-    src, dst, coef, silu, slope, q_v, acc, res, dyn,
+    src, dst, coef, silu, slope, side, q_v, acc, res, dyn,
     load_sem, send_sem, recv_sem, psend, precv,
 ):
     nseq = lax.axis_size("seq")
@@ -58,20 +59,20 @@
         (lg_h.at[0], lg_v),
     )
     loads = [pltpu.make_async_copy(a, b, load_sem.at[i]) for i, (a, b) in enumerate(pairs)]
-    for c in loads:
+    for c in loads[:4]:
         c.start()
 
     barrier = pltpu.get_barrier_semaphore()
 
-    def greet(j, carry):
-        pl.semaphore_signal(
-            barrier, inc=1, device_id={"seq": lax.rem(me + j, nseq)}, device_id_type=MESH
-        )
-        return carry
-
-    lax.fori_loop(1, nseq, greet, 0)
+    for d in range(nseq // 2, 0, -1):
+        for peer in sorted({(nseq + d) % nseq, (nseq - d) % nseq}):
+            pl.semaphore_signal(
+                barrier, inc=1, device_id={"seq": lax.rem(me + peer, nseq)}, device_id_type=MESH
+            )
     for other in (before, after):
         pl.semaphore_signal(barrier, inc=1, device_id={"pipe": other}, device_id_type=MESH)
+    for c in loads[4:]:
+        c.start()
 
     def copy_to(a, n, peer):
         return pltpu.make_async_remote_copy(
@@ -84,13 +85,15 @@
         )
 
     def send(a, n):
+        half = nseq // 2
+        copy_to(a, n, lax.rem(me + half, nseq)).start()
+
         def body(j, carry):
-            copy_to(a, n, lax.rem(me + j, nseq)).start()
-            copy_to(a, n, lax.rem(me + nseq - j, nseq)).start()
+            copy_to(a, n, lax.rem(me + half + j, nseq)).start()
+            copy_to(a, n, lax.rem(me + half - j, nseq)).start()
             return carry
 
-        lax.fori_loop(1, nseq // 2, body, 0)
-        copy_to(a, n, lax.rem(me + nseq // 2, nseq)).start()
+        lax.fori_loop(1, half, body, 0)
         dst[a, n, me] = src[a, n, me]
 
     def whole(a, n):
@@ -112,12 +115,12 @@
     def cols(n):
         return pl.ds(pl.multiple_of(n * width, 128), width)
 
-    def each(body):
+    def each(body, first=0):
         def step(n, carry):
             body(n)
             return carry
 
-        lax.fori_loop(0, NBLK, step, 0)
+        lax.fori_loop(first, NBLK, step, 0)
 
     def scale_of(t):
         total = jnp.zeros((rows, 1), F32)
@@ -215,12 +218,12 @@
         acc[...] = jnp.zeros_like(acc)
 
         def part(n):
+            whole(v, n).wait_recv()
+            value_grad = dot_nn(rt_v[...], take(v, n).astype(BF16)).astype(BF16)
+            side[...] = dot_nt(value_grad, wv_v[:, cols(n)])
             whole(m, n).wait_recv()
             gate_grad = (coef[n] * take(m, n)).astype(BF16)
-            left = dot_nt(gate_grad, wg_v[:, cols(n)])
-            whole(v, n).wait_recv()
-            value_grad = dot_nn(rt_v[...], take(v, n).astype(BF16)).astype(BF16)
-            e = (left + dot_nt(value_grad, wv_v[:, cols(n)])) * gain_v[:, cols(n)]
+            e = (dot_nt(gate_grad, wg_v[:, cols(n)]) + side[...]) * gain_v[:, cols(n)]
             base[n] = dy_v[:, cols(n)].astype(F32) + q_v[t] * e
             acc[...] += jnp.sum(e * x_v[t][:, cols(n)].astype(F32), axis=-1, keepdims=True)
 
@@ -259,20 +262,24 @@
         put(G1, n, inner * silu[n])
         coef[n] = inner * slope[n]
         send(G1, n)
-        mix(A1, M1, n)
+
+        @pl.when(n < NBLK - HELD)
+        def _():
+            mix(A1, M1, n)
 
     each(start1)
     each(functools.partial(fold, G1, V1))
+    each(functools.partial(mix, A1, M1), NBLK - HELD)
 
     def drain(a, n):
         whole(a, n).wait_send()
 
-    for a in range(7):
+    for a in (A0, G0, M0, V0, A1, G1, V1):
         each(functools.partial(drain, a))
     each(lambda n: passing(n).wait_send())
     finish(1, M1, V1)
     weight[...] = jnp.broadcast_to(acc[...], weight.shape)
-    each(functools.partial(drain, V1))
+    each(functools.partial(drain, M1))
 
 
 def closing(out0, x1_v, base, weight, out_h, res, out_sem):
@@ -328,6 +335,7 @@
             vmem((NBLK, rows, width), F32),
             vmem((NBLK, rows, width), F32),
             vmem((NBLK, rows, width), F32),
+            vmem((rows, width), F32),
             vmem((ticks, rows, 1), F32),
             vmem((rows, 1), F32),
             vmem((NBLK, rows, width), BF16),

time: 150 us -> 149 us (level)
  no operation moved by 1% of the time
where the time goes in v3:
time: 149 us
  Pallas kernels  149 us (100%)
    pallas_call x1, Pallas kernels, local(): pl.pallas_call(kernel, out_shape=(vmem((rows, model), BF16), vmem((rows,...  148 us

profile of v3, /device:TPU:2, one launch (start us, length us, event | category | flops | bytes accessed | tf_op | source)
XLA Modules:
  0.0 149.0 jit_solution(3120530941749154902)
XLA Ops:
  0.0 147.8 %shard_map.91 = (bf16[256,1536]{1,0:T(8,128)(2,1)S(1)}, bf16[256,1536]{1,0:T(8,128)(2,1)S(1)}, f32[4,256,384]{2,1,0:T(8,128)S(1)}, f32[256,128]{1,0:T(8,128)S(1)}) custom-call(bf16[1,2,256,1536]{3,2,1,0:T(8,128)(2,1)} %x_h.1, bf16[1,256,1536]{2,1,0:T(8,128)(2,1)} %dy_h.1, bf16[1,256,1536]{2,1,0:T(8,128)(2,1)} %lg_h.1, f32[1,1536]{1,0:T(1,128)} %gain_h.1, ...), custom_call_target="tpu_custom_call" | custom-call | tf_op jit(solution)/shard_map/pallas_call | solution.py:310
  147.8 1.2 shard_map.92

commit v4 on v3

--- a/solution.py
+++ b/solution.py
@@ -31,7 +31,7 @@
     x_h, dy_h, lg_h, gain_h, wg_h, wv_h, wo_h, r_h, l_h,
     out0, x1_v, base, weight,
     x0_v, dy_v, lg_v, gain_v, wg_v, wv_v, wo_v, r_v, rt_v, l_v, lb_v, lbt_v,
-    src, dst, coef, silu, slope, side, q_v, acc, res, dyn,
+    src, dst, coef, silu, slope, side, gx, qg, q_v, acc, res, dyn,
     load_sem, send_sem, recv_sem, psend, precv,
 ):
     nseq = lax.axis_size("seq")
@@ -221,11 +221,16 @@
             whole(v, n).wait_recv()
             value_grad = dot_nn(rt_v[...], take(v, n).astype(BF16)).astype(BF16)
             side[...] = dot_nt(value_grad, wv_v[:, cols(n)])
+            scaled = gain_v[:, cols(n)] * x_v[t][:, cols(n)].astype(F32)
+            gx[...] = scaled
+            acc[...] += jnp.sum(side[...] * scaled, axis=-1, keepdims=True)
+            qg[...] = q_v[t] * gain_v[:, cols(n)]
+            base[n] = dy_v[:, cols(n)].astype(F32) + qg[...] * side[...]
             whole(m, n).wait_recv()
             gate_grad = (coef[n] * take(m, n)).astype(BF16)
-            e = (dot_nt(gate_grad, wg_v[:, cols(n)]) + side[...]) * gain_v[:, cols(n)]
-            base[n] = dy_v[:, cols(n)].astype(F32) + q_v[t] * e
-            acc[...] += jnp.sum(e * x_v[t][:, cols(n)].astype(F32), axis=-1, keepdims=True)
+            e = dot_nt(gate_grad, wg_v[:, cols(n)])
+            base[n] += qg[...] * e
+            acc[...] += jnp.sum(e * gx[...], axis=-1, keepdims=True)
 
         each(part)
         q = q_v[t]
@@ -335,6 +340,8 @@
             vmem((NBLK, rows, width), F32),
             vmem((NBLK, rows, width), F32),
             vmem((NBLK, rows, width), F32),
+            vmem((rows, width), F32),
+            vmem((rows, width), F32),
             vmem((rows, width), F32),
             vmem((ticks, rows, 1), F32),
             vmem((rows, 1), F32),

time: 149 us -> 149 us (level)
  no operation moved by 1% of the time
where the time goes in v4:
time: 149 us
  Pallas kernels  149 us (100%)
    pallas_call x1, Pallas kernels, local(): pl.pallas_call(kernel, out_shape=(vmem((rows, model), BF16), vmem((rows,...  148 us

profile of v4, /device:TPU:2, one launch (start us, length us, event | category | flops | bytes accessed | tf_op | source)
XLA Modules:
  0.0 149.0 jit_solution(10452289637628149662)
XLA Ops:
  0.0 147.8 %shard_map.91 = (bf16[256,1536]{1,0:T(8,128)(2,1)S(1)}, bf16[256,1536]{1,0:T(8,128)(2,1)S(1)}, f32[4,256,384]{2,1,0:T(8,128)S(1)}, f32[256,128]{1,0:T(8,128)S(1)}) custom-call(bf16[1,2,256,1536]{3,2,1,0:T(8,128)(2,1)} %x_h.1, bf16[1,256,1536]{2,1,0:T(8,128)(2,1)} %dy_h.1, bf16[1,256,1536]{2,1,0:T(8,128)(2,1)} %lg_h.1, f32[1,1536]{1,0:T(1,128)} %gain_h.1, ...), custom_call_target="tpu_custom_call" | custom-call | tf_op jit(solution)/shard_map/pallas_call | solution.py:315
  147.8 1.2 shard_map.92

commit v5 on v4

--- a/solution.py
+++ b/solution.py
@@ -10,6 +10,7 @@
 TICKS = 2
 NBLK = 4
 HELD = 2
+NEAR = 3
 MESH = pl.DeviceIdType.MESH
 F32 = jnp.float32
 BF16 = jnp.bfloat16
@@ -86,14 +87,15 @@
 
     def send(a, n):
         half = nseq // 2
-        copy_to(a, n, lax.rem(me + half, nseq)).start()
 
         def body(j, carry):
             copy_to(a, n, lax.rem(me + half + j, nseq)).start()
             copy_to(a, n, lax.rem(me + half - j, nseq)).start()
             return carry
 
-        lax.fori_loop(1, half, body, 0)
+        lax.fori_loop(half - NEAR, half, body, 0)
+        copy_to(a, n, lax.rem(me + half, nseq)).start()
+        lax.fori_loop(1, half - NEAR, body, 0)
         dst[a, n, me] = src[a, n, me]
 
     def whole(a, n):

time: 149 us -> 149 us (level)
  no operation moved by 1% of the time
where the time goes in v5:
time: 149 us
  Pallas kernels  149 us (100%)
    pallas_call x1, Pallas kernels, local(): pl.pallas_call(kernel, out_shape=(vmem((rows, model), BF16), vmem((rows,...  148 us

profile of v5, /device:TPU:2, one launch (start us, length us, event | category | flops | bytes accessed | tf_op | source)
XLA Modules:
  0.0 149.0 jit_solution(17545298270965032146)
XLA Ops:
  0.0 147.8 %shard_map.91 = (bf16[256,1536]{1,0:T(8,128)(2,1)S(1)}, bf16[256,1536]{1,0:T(8,128)(2,1)S(1)}, f32[4,256,384]{2,1,0:T(8,128)S(1)}, f32[256,128]{1,0:T(8,128)S(1)}) custom-call(bf16[1,2,256,1536]{3,2,1,0:T(8,128)(2,1)} %x_h.1, bf16[1,256,1536]{2,1,0:T(8,128)(2,1)} %dy_h.1, bf16[1,256,1536]{2,1,0:T(8,128)(2,1)} %lg_h.1, f32[1,1536]{1,0:T(1,128)} %gain_h.1, ...), custom_call_target="tpu_custom_call" | custom-call | tf_op jit(solution)/shard_map/pallas_call | solution.py:317
  147.8 1.2 shard_map.92
